TPU v7x, 32 devices: a whole 2x2x4 slice. The times are simulated.
32 devices in a mesh: batch: 4 (over z), ctx: 2 (over x), tp: 4 (over y, core).
Axes of the slice: x: 2, y: 2, z: 4, core: 2. Of those that a mesh axis runs over, the one named last changes fastest.
Arguments:
- hits: bfloat16 [2048, 1024], P(('batch', 'ctx'), 'tp'), parts along dimension 0, may hold values from -12 to 12
- qkv_weight: bfloat16 [1024, 3, 1024], P(None, None, 'tp'), may hold values from -0.75 to 0.75
- out_weight: bfloat16 [1024, 1024], P('tp'), may hold values from -0.1875 to 0.1875
- energy_order: int32 [2048], P('batch'), parts along dimension 0, may hold values from 0 to 511, as said below
- stripe_owner: int32 [8, 2], P('batch'), parts along dimension 0, may hold values from 0 to 3, as said below
Outputs:
- mixed: bfloat16 [8, 256, 1024], P(('batch', 'ctx'), 'tp'), parts along dimension 0
There are 4 independent parts, one for each index of `batch`. A program takes and returns all parts, laid end to end along the dimension named above; an argument that names none is the same for every part. Nothing has to cross between parts.
Inputs may be any that keep to these rules, and one draw needn't show every extreme that they name: `energy_order`: a permutation of the 512 detector rows; every stripe of 128 consecutive energy positions holds exactly 64 hits of each block of 256 consecutive detector rows. `stripe_owner`: each row holds two stripes a and 3 - a, in either order; every stripe appears exactly once.
All inputs are finite; a program needn't handle non-finite values.
Results may differ from a plain program's by a relative error of at most 0.012.
The roundings to bfloat16 on the way count: a program that leaves them out, or rounds other values in their place, can miss the bound.
Values may be sent and summed in bfloat16 or wider, within the bound.
A program may use at most 64 MiB of HBM per device.

v0:
```python
import math

import jax
import jax.numpy as jnp
from jax import lax
from jax.sharding import PartitionSpec as P

HEAD_DIM = 64


floor_score = -1e30


def passed_along(shard, axis, by):
    peers = lax.axis_size(axis)
    return lax.ppermute(shard, axis, [(i, (i + by) % peers) for i in range(peers)])


def stripe_rows(owners, rows_dev, stripes):
    stripe_len = rows_dev // 2
    offsets = jnp.arange(stripe_len, dtype=jnp.int32)
    low_rows = owners[:, None] * stripe_len + offsets[None, :]
    high_rows = (stripes - 1 - owners)[:, None] * stripe_len + offsets[None, :]
    return jnp.concatenate([low_rows, high_rows], axis=1)


def routing(energy_order, pair_owner, my_index, rows_dev, count_ctx):
    every_row = stripe_rows(pair_owner, rows_dev, 2 * count_ctx)
    detector = energy_order[every_row]
    source = detector // rows_dev
    chosen = (source == my_index).astype(jnp.int32)
    ranked = jnp.cumsum(chosen, axis=1) - 1
    per_pair = rows_dev // count_ctx
    slot_ids = jnp.arange(per_pair, dtype=jnp.int32)
    matched = (chosen[:, None, :] == 1) & (ranked[:, None, :] == slot_ids[None, :, None])
    send_rows = jnp.sum(jnp.where(matched, (detector % rows_dev)[:, None, :], 0), axis=-1)
    my_positions = lax.dynamic_index_in_dim(every_row, my_index, 0, keepdims=False)
    mine_source = energy_order[my_positions] // rows_dev
    onehot = (mine_source[:, None] == jnp.arange(count_ctx, dtype=jnp.int32)[None, :]).astype(
        jnp.int32
    )
    mine_rank = jnp.sum((jnp.cumsum(onehot, axis=0) - 1) * onehot, axis=1)
    return (send_rows.reshape(-1), mine_source * per_pair + mine_rank, my_positions)


def empty_state(heads_dev, count_rows):
    return (
        jnp.full((heads_dev, count_rows), floor_score, jnp.float32),
        jnp.zeros((heads_dev, count_rows), jnp.float32),
        jnp.zeros((count_rows, heads_dev, HEAD_DIM), jnp.float32),
    )


def absorb(state_now, queries, key_rows, value_rows, allowed, score_scale):
    running_max, running_sum, running_acc = state_now
    scores = (
        jnp.einsum("qhe,khe->hqk", queries, key_rows, preferred_element_type=jnp.float32)
        * score_scale
    )
    if allowed is not None:
        scores = jnp.where(allowed[None], scores, floor_score)
    new_max = jnp.maximum(running_max, jnp.max(scores, axis=-1))
    weights = jnp.exp(scores - new_max[:, :, None])
    if allowed is not None:
        weights = jnp.where(allowed[None], weights, 0.0)
    shrink = jnp.exp(running_max - new_max)
    new_sum = running_sum * shrink + jnp.sum(weights, axis=-1)
    added = jnp.einsum(
        "hqk,khe->qhe", weights.astype(jnp.bfloat16), value_rows, preferred_element_type=jnp.float32
    )
    new_acc = running_acc * jnp.transpose(shrink)[:, :, None] + added
    return (new_max, new_sum, new_acc)


def finish(state_now):
    return state_now[2] / jnp.transpose(state_now[1])[:, :, None]


def shards(hits, qkv_weight, out_weight, energy_order, stripe_owner):
    rows_dev, width_dev = hits.shape
    model_width = qkv_weight.shape[0]
    count_ctx = lax.axis_size("ctx")
    my_index = lax.axis_index("ctx")
    heads_dev = width_dev // HEAD_DIM
    score_scale = 1.0 / math.sqrt(HEAD_DIM)
    stripe_len = rows_dev // 2
    per_pair = rows_dev // count_ctx
    pair_owner = jnp.minimum(stripe_owner[:, 0], stripe_owner[:, 1])
    send_rows, take_rows, my_positions = routing(
        energy_order, pair_owner, my_index, rows_dev, count_ctx
    )
    flat_weight = qkv_weight.reshape(model_width, 3 * width_dev)
    outgoing = hits[send_rows].reshape(count_ctx, per_pair, width_dev)
    incoming = lax.all_to_all(outgoing, "ctx", split_axis=0, concat_axis=0, tiled=True)
    arranged = incoming.reshape(count_ctx * per_pair, width_dev)[take_rows]
    projected = jnp.dot(
        lax.all_gather(arranged, "tp", axis=1, tiled=True),
        flat_weight,
        preferred_element_type=jnp.float32,
    ).astype(jnp.bfloat16)
    queries = projected[:, :width_dev].reshape(rows_dev, heads_dev, HEAD_DIM)
    key_value = projected[:, width_dev:]
    low_queries = queries[:stripe_len]
    high_queries = queries[stripe_len:]

    def split_pair(pair_block):
        count_rows = pair_block.shape[0]
        return (
            pair_block[:, :width_dev].reshape(count_rows, heads_dev, HEAD_DIM),
            pair_block[:, width_dev:].reshape(count_rows, heads_dev, HEAD_DIM),
        )

    my_stripe = pair_owner[my_index]
    own_keys, own_values = split_pair(key_value)
    low_allowed = my_positions[None, :stripe_len] <= my_positions[:stripe_len, None]
    high_allowed = my_positions[None, :] <= my_positions[stripe_len:, None]
    low_state = absorb(
        empty_state(heads_dev, stripe_len),
        low_queries,
        own_keys[:stripe_len],
        own_values[:stripe_len],
        low_allowed,
        score_scale,
    )
    high_state = absorb(
        empty_state(heads_dev, stripe_len),
        high_queries,
        own_keys,
        own_values,
        high_allowed,
        score_scale,
    )

    def advance(turn_index, state_now):
        pair_block, low_now, high_now = state_now
        pair_block = passed_along(pair_block, "ctx", 1)
        sender = (my_index - turn_index) % count_ctx
        their_stripe = pair_owner[sender]
        key_rows, value_rows = split_pair(pair_block)
        high_now = absorb(
            high_now,
            high_queries,
            key_rows[:stripe_len],
            value_rows[:stripe_len],
            None,
            score_scale,
        )

        def lower_first():
            return (
                absorb(
                    low_now,
                    low_queries,
                    key_rows[:stripe_len],
                    value_rows[:stripe_len],
                    None,
                    score_scale,
                ),
                high_now,
            )

        def upper_first():
            return (
                low_now,
                absorb(
                    high_now,
                    high_queries,
                    key_rows[stripe_len:],
                    value_rows[stripe_len:],
                    None,
                    score_scale,
                ),
            )

        low_now, high_now = lax.cond(their_stripe < my_stripe, lower_first, upper_first)
        return (pair_block, low_now, high_now)

    moved_block, low_state, high_state = lax.fori_loop(
        1, count_ctx, advance, (key_value, low_state, high_state)
    )
    attended = jnp.concatenate([finish(low_state), finish(high_state)], axis=0)
    merged = attended.astype(jnp.bfloat16).reshape(rows_dev, width_dev)
    my_pair = stripe_owner[my_index]
    swapped = my_pair[0] > my_pair[1]
    merged = jnp.where(swapped, jnp.roll(merged, stripe_len, axis=0), merged)
    mixed = lax.psum_scatter(
        jnp.dot(merged, out_weight, preferred_element_type=jnp.float32).astype(jnp.bfloat16),
        "tp",
        scatter_dimension=0,
        tiled=True,
    )
    return mixed[None]


def solution(mesh):
    placed = (
        P(("batch", "ctx"), "tp"),
        P(None, None, "tp"),
        P("tp", None),
        P("batch"),
        P("batch", None),
    )
    return jax.shard_map(
        shards,
        mesh=mesh,
        in_specs=placed,
        out_specs=P(("batch", "ctx"), "tp", None),
        check_vma=False,
    )
```

profile of v0, /device:TPU:0, one launch (start us, length us, event | category | flops | bytes accessed | tf_op | source)
XLA Modules:
  0.0 79.0 jit_solution(4535081278310900009)
XLA Ops:
  6.5 1.0 %multiply_reduce_fusion.1 = (s32[2]{0:T(128)S(1)}, s32[2]{0:T(128)S(1)}, s32[2,1]{1,0:T(2,128)S(1)}) fusion(s32[2,2]{1,0:T(2,128)} %param.11), kind=kLoop, calls=%fused_computation.137 | loop fusion | flops 8 | bytes 40 | tf_op jit(solution)/shard_map/mul | solution.py:22
  7.7 2.0 %gather_fusion.2 = s32[256]{0:T(256)S(1)} fusion(s32[512]{0:T(512)} %param.10, s32[1024]{0:T(1024)S(1)} %pad_clamp_fusion.1), kind=kCustom, calls=%fused_computation.2 | custom fusion | bytes 3072 | tf_op jit(solution)/shard_map/gather | solution.py:38
  9.8 3.5 %gather_fusion = s32[512]{0:T(512)S(1)} fusion(s32[512]{0:T(512)S(1)} %copy-done.1, s32[1024]{0:T(1024)S(1)} %pad_clamp_fusion.3), kind=kCustom, calls=%fused_computation | custom fusion | bytes 6144 | tf_op jit(solution)/shard_map/gather | solution.py:29
  13.4 0.6 reduce-window.16
  14.0 0.2 slice_reduce_fusion
  14.2 0.2 reduce-window.19
  14.5 0.6 reduce-window.14
  15.1 0.2 slice_reduce_fusion.1
  15.4 0.2 reduce-window.15
  15.6 0.1 select_reduce_fusion
  15.8 1.8 %gather_fusion.1 = bf16[256,256]{1,0:T(8,128)(2,1)} fusion(bf16[256,256]{1,0:T(8,128)(2,1)S(1)} %copy-done.2, s32[1024]{0:T(1024)S(1)} %pad_clamp_fusion.2), kind=kCustom, calls=%fused_computation.1 | custom fusion | bytes 263168 | tf_op jit(solution)/shard_map/gather | solution.py:93
  17.6 4.2 %all-to-all-start = ((bf16[2,128,256]{2,1,0:T(8,128)(2,1)}), bf16[2,128,256]{2,1,0:T(8,128)(2,1)S(1)}, u32[]{:S(2)}, u32[]{:S(2)}) async-start(bf16[2,128,256]{2,1,0:T(8,128)(2,1)} %bitcast.11), calls=%async_computation | async-start | bytes 262144 | tf_op jit(solution)/shard_map/all_to_all | solution.py:94
  21.9 0.6 constant_dynamic-slice_fusion
  23.8 1.8 %copy.51 = bf16[1024,3,256]{0,2,1:T(8,128)(2,1)} copy(bf16[1024,3,256]{2,0,1:T(8,128)(2,1)S(1)} %copy-done.3) | data formatting | bytes 3145728 | tf_op args[1]
  25.6 0.6 fusion.67
  27.6 1.2 %gather_fusion.3 = bf16[256,256]{1,0:T(8,128)(2,1)S(1)} fusion(bf16[256,256]{1,0:T(8,128)(2,1)S(1)} %bitcast.118, s32[1024]{0:T(1024)S(1)} %pad_clamp_fusion), kind=kCustom, calls=%fused_computation.3 | custom fusion | bytes 263168 | tf_op jit(solution)/shard_map/gather | solution.py:95
  28.8 7.9 %all-gather = bf16[256,1024]{1,0:T(8,128)(2,1)S(1)} all-gather(bf16[256,256]{1,0:T(8,128)(2,1)S(1)} %gather_fusion.3), channel_id=2, replica_groups=mesh['batch'=4,'ctx'=2,'tp'=4] {'tp'}, dimensions={1}, use_global_device_ids=true | all-gather | bytes 655360 | tf_op jit(solution)/shard_map/all_gather | solution.py:97
  36.7 0.6 convolution_convert_fusion.1
  37.4 2.0 %collective-permute-start = (bf16[256,512]{1,0:T(8,128)(2,1)S(1)}, bf16[256,512]{1,0:T(8,128)(2,1)S(1)}, u32[]{:S(2)}, u32[]{:S(2)}) collective-permute-start(bf16[256,512]{1,0:T(8,128)(2,1)S(1)} %slice.177), channel_id=1, source_target_pairs={{0,4},{4,0},{1,5},{5,1},{2,6},{6,2},{3,7},{7,3},{8,12},{12,8},{9,1... | collective-permute-start | bytes 786440 | tf_op jit(solution)/shard_map/while/body/eval_jaxpr/ppermute | solution.py:16
  39.6 0.3 fusion.70
  40.1 0.2 fusion.20
  40.6 0.3 fusion.68
  41.0 5.2 %collective-permute-done = bf16[256,512]{1,0:T(8,128)(2,1)S(1)} collective-permute-done((bf16[256,512]{1,0:T(8,128)(2,1)S(1)}, bf16[256,512]{1,0:T(8,128)(2,1)S(1)}, u32[]{:S(2)}, u32[]{:S(2)}) %collective-permute-start) | collective-permute-done | bytes 262176 | tf_op jit(solution)/shard_map/while/body/eval_jaxpr/ppermute | solution.py:16
  46.3 0.3 fusion.69
  47.0 0.3 fusion.23
  47.3 0.3 fusion.19
  47.6 0.2 fusion.21
  47.8 0.6 conditional.1
  47.8 0.3 fusion.61
  48.1 0.2 fusion
  48.4 1.1 %convolution_convert_fusion = bf16[256,1024]{1,0:T(8,128)(2,1)} fusion(bf16[256,1024]{1,0:T(8,128)(2,1)S(1)} %copy-done, bf16[128,256]{0,1:T(8,128)(2,1)S(1)} %bitcast.135, bf16[128,256]{0,1:T(8,128)(2,1)S(1)} %bitcast.136, pred[]{:T(512)} %bitcast.4), kind=kOutput, calls=%fused_computation.28 | convolution fusion | flops 135069696 | bytes 1179649 | tf_op jit(solution)/shard_map/dot_general | solution.py:187
  49.5 22.6 %reduce-scatter.2.cloned.1.call-done = bf16[64,1024]{1,0:T(8,128)(2,1)} async-done(((bf16[256,1024]{1,0:T(8,128)(2,1)}), bf16[64,1024]{1,0:T(8,128)(2,1)}) %reduce-scatter.2.cloned.1.call-update) | async-done | bytes 131088 | tf_op jit(solution)/shard_map/reduce_scatter | solution.py:186
  (67 shorter events, 2.2 us)
Async XLA Ops:
  6.5 41.8 %copy-start = (bf16[256,1024]{1,0:T(8,128)(2,1)S(1)}, bf16[256,1024]{1,0:T(8,128)(2,1)}, u32[]{:S(2)}) copy-start(bf16[256,1024]{1,0:T(8,128)(2,1)} %param.9) | copy-start | bytes 1572868
  6.5 3.3 %copy-start.1 = (s32[512]{0:T(512)S(1)}, s32[512]{0:T(512)}, u32[]{:S(2)}) copy-start(s32[512]{0:T(512)} %param.10) | copy-start | bytes 6148
  7.7 8.1 %copy-start.2 = (bf16[256,256]{1,0:T(8,128)(2,1)S(1)}, bf16[256,256]{1,0:T(8,128)(2,1)}, u32[]{:S(2)}) copy-start(bf16[256,256]{1,0:T(8,128)(2,1)} %param.7) | copy-start | bytes 393220
  9.8 12.1 %copy-start.5 = (s32[2,2]{1,0:T(2,128)S(1)}, s32[2,2]{1,0:T(2,128)}, u32[]{:S(2)}) copy-start(s32[2,2]{1,0:T(2,128)} %param.11) | copy-start | bytes 52
  9.8 13.9 %copy-start.3 = (bf16[1024,3,256]{2,0,1:T(8,128)(2,1)S(1)}, bf16[1024,3,256]{2,0,1:T(8,128)(2,1)}, u32[]{:S(2)}) copy-start(bf16[1024,3,256]{2,0,1:T(8,128)(2,1)} %param.8) | copy-start | bytes 4718596
  17.6 10.0 %all-to-all-start = ((bf16[2,128,256]{2,1,0:T(8,128)(2,1)}), bf16[2,128,256]{2,1,0:T(8,128)(2,1)S(1)}, u32[]{:S(2)}, u32[]{:S(2)}) async-start(bf16[2,128,256]{2,1,0:T(8,128)(2,1)} %bitcast.11), calls=%async_computation | async-start | bytes 262144 | tf_op jit(solution)/shard_map/all_to_all | solution.py:94
  21.9 50.3 %reduce-scatter.2.cloned.1.call-start = ((), (), s32[]{:S(2)}) async-start(), calls=%async_computation.2 | async-start | bytes 655360 | tf_op jit(solution)/shard_map/reduce_scatter | solution.py:186
  25.5 11.2 %copy-start.4 = (bf16[1024,3,256]{0,2,1:T(8,128)(2,1)S(1)}, bf16[1024,3,256]{0,2,1:T(8,128)(2,1)}, u32[]{:S(2)}) copy-start(bf16[1024,3,256]{0,2,1:T(8,128)(2,1)} %copy.51) | copy-start | bytes 4718596
  37.4 8.8 %collective-permute-start = (bf16[256,512]{1,0:T(8,128)(2,1)S(1)}, bf16[256,512]{1,0:T(8,128)(2,1)S(1)}, u32[]{:S(2)}, u32[]{:S(2)}) collective-permute-start(bf16[256,512]{1,0:T(8,128)(2,1)S(1)} %slice.177), channel_id=1, source_target_pairs={{0,4},{4,0},{1,5},{5,1},{2,6},{6,2},{3,7},{7,3},{8,12},{12,8},{9,1... | collective-permute-start | bytes 786440 | tf_op jit(solution)/shard_map/while/body/eval_jaxpr/ppermute | solution.py:16
Sparse Core Ops, SparseCore 0:
  49.7 22.4 reduce-scatter.1
where the time goes:
time: 79.2 us; the launch traced here: 79 us
  waiting for transfers between devices  27.8 us (35%)
  between operations  16.3 us (21%)
  local copies, waits for them, and re-layouts  13.1 us (17%)
  blocking collectives  7.91 us (10%)
  starting transfers between devices  6.22 us (8%)
  other arithmetic  3.88 us (5%)
  matrix products  3.68 us (5%)
    reduce_scatter x1, waiting for transfers between devices, shards(): lax.psum_scatter(jnp.dot(merged, out_weight, preferred_element_type=jnp.f...  22.6 us
    all_gather x1, blocking collectives, shards(): lax.all_gather(arranged, 'tp', axis=1, tiled=True)  7.91 us
    ppermute x1, waiting for transfers between devices, passed_along(): lax.ppermute(shard, axis, [(i, (i + by) % peers) for i in range(peers)])  5.22 us
    all_to_all x1, starting transfers between devices, shards(): lax.all_to_all(outgoing, 'ctx', split_axis=0, concat_axis=0, tiled=True)  4.23 us
    gather x2, local copies, waits for them, and re-layouts, routing(): detector = energy_order[every_row]  3.51 us
    gather x1, local copies, waits for them, and re-layouts, routing(): mine_source = energy_order[my_positions] // rows_dev  2.03 us
    ppermute x1, starting transfers between devices, passed_along(): lax.ppermute(shard, axis, [(i, (i + by) % peers) for i in range(peers)])  1.99 us
    gather x1, local copies, waits for them, and re-layouts, shards(): outgoing = hits[send_rows].reshape(count_ctx, per_pair, width_dev)  1.81 us
  transfers between devices with their start and end apart: 3, of which 2 were waited for; matrix products, arithmetic and copies ran while one was open for 6% of the time, Pallas kernels for 0%

commit v1 on v0

--- a/solution.py
+++ b/solution.py
@@ -3,6 +3,8 @@
 import jax
 import jax.numpy as jnp
 from jax import lax
+from jax.experimental import pallas as pl
+from jax.experimental.pallas import tpu as pltpu
 from jax.sharding import PartitionSpec as P
 
 HEAD_DIM = 64
@@ -192,7 +194,292 @@
     return mixed[None]
 
 
+def layer_kernel(
+    hits_ref,
+    qkv_ref,
+    wout_ref,
+    order_ref,
+    owner_ref,
+    out_ref,
+    gath,
+    wq,
+    wmine,
+    wtheirs,
+    acc,
+    proj,
+    pick,
+    bias,
+    qrows,
+    att_send,
+    att_recv,
+    far_send,
+    far_recv,
+    near,
+    local_sem,
+    send_sem,
+    gath_sem,
+    wout_sem,
+    att_sem,
+    far_sem,
+):
+    i = lax.axis_index("ctx")
+    t = lax.axis_index("tp")
+    y = t // 2
+    c = t % 2
+    oi, oy = 1 - i, 1 - y
+    rows, width = hits_ref.shape
+    seq = 2 * rows
+    half = rows // 2
+    quarter = rows // 4
+    heads = width // HEAD_DIM
+    score_scale = 1.0 / math.sqrt(HEAD_DIM)
+    partner = {"ctx": i, "tp": 2 * y + 1 - c}
+    x_peer = {"ctx": oi, "tp": t}
+    y_peer = {"ctx": i, "tp": 2 * oy + c}
+    t_partner = 2 * y + 1 - c
+    t_y = 2 * oy + c
+    t_diag_partner = 2 * oy + 1 - c
+
+    local = []
+
+    def local_copy(src, dst):
+        copy = pltpu.make_async_copy(src, dst, local_sem.at[len(local)])
+        copy.start()
+        local.append(copy)
+        return copy
+
+    hits_in = local_copy(hits_ref, gath.at[i, t])
+    weight_in = [
+        [
+            local_copy(
+                qkv_ref.at[j, pl.ds(part * 2 * width, 2 * width)],
+                wq.at[j, pl.ds(part * 2 * width, 2 * width)],
+            )
+            for j in range(3)
+        ]
+        for part in (y, oy)
+    ]
+    wout_in = local_copy(wout_ref, wmine)
+
+    barrier = pltpu.get_barrier_semaphore()
+    for peer in (partner, x_peer, y_peer):
+        pl.semaphore_signal(
+            barrier, inc=1, device_id=peer, device_id_type=pl.DeviceIdType.MESH
+        )
+    pl.semaphore_wait(barrier, 3)
+
+    sent = []
+
+    def remote(src, dst, recv, peer):
+        copy = pltpu.make_async_remote_copy(
+            src_ref=src,
+            dst_ref=dst,
+            send_sem=send_sem.at[len(sent)],
+            recv_sem=recv,
+            device_id=peer,
+            device_id_type=pl.DeviceIdType.MESH,
+        )
+        copy.start()
+        sent.append(copy)
+
+    def arrived(dst, recv):
+        pltpu.make_async_remote_copy(
+            src_ref=dst,
+            dst_ref=dst,
+            send_sem=send_sem.at[0],
+            recv_sem=recv,
+            device_id=partner,
+            device_id_type=pl.DeviceIdType.MESH,
+        ).wait_recv()
+
+    def slot(ci, ti, h):
+        return gath.at[ci, ti, pl.ds(h * half, half)]
+
+    def own_to(h, peer):
+        remote(hits_ref.at[pl.ds(h * half, half)], slot(i, t, h), gath_sem.at[i, t, h], peer)
+
+    def forward(ci, ti, h, peer):
+        remote(slot(ci, ti, h), slot(ci, ti, h), gath_sem.at[ci, ti, h], peer)
+
+    def got(ci, ti, h):
+        arrived(slot(ci, ti, h), gath_sem.at[ci, ti, h])
+
+    own_to(0, x_peer)
+    own_to(1, y_peer)
+    own_to(0, partner)
+    own_to(1, partner)
+    own_to(1, x_peer)
+    own_to(0, y_peer)
+    remote(wout_ref, wtheirs, wout_sem.at[0], partner)
+
+    order = order_ref[...].astype(jnp.float32)
+    order_rows = jnp.transpose(jnp.broadcast_to(order, (128, seq)))
+    entry = lax.broadcasted_iota(jnp.int32, (seq, 128), 0).astype(jnp.float32)
+    lane = lax.broadcasted_iota(jnp.int32, (seq, 128), 1)
+    row = lax.broadcasted_iota(jnp.int32, (rows, 128), 0)
+    first, second = owner_ref[i, 0], owner_ref[i, 1]
+    mine_pos = jnp.where(row < half, first * half + row, second * half + row - half).astype(
+        jnp.float32
+    )
+    for block in range(seq // 128):
+        cols = pl.ds(block * 128, 128)
+        detector = (lane + block * 128).astype(jnp.float32)
+        pos = jnp.sum(jnp.where(order_rows == detector, entry, 0.0), axis=0, keepdims=True)
+        bias[:, cols] = jnp.where(pos <= mine_pos, 0.0, floor_score)
+        pick[:, cols] = jnp.where(pos == mine_pos, score_scale, 0.0).astype(jnp.bfloat16)
+
+    def partial(ci, part, j):
+        left = jnp.concatenate([gath[ci, 2 * part], gath[ci, 2 * part + 1]], axis=1)
+        right = wq[j, pl.ds(pl.multiple_of(part * 2 * width, 2 * width), 2 * width), :]
+        return jnp.dot(left, right, preferred_element_type=jnp.float32)
+
+    def open_rows(ci, which):
+        for j in range(3):
+            acc[which, j] = partial(ci, y, j)
+
+    def close_rows(ci, which):
+        for j in range(3):
+            proj[j, pl.ds(pl.multiple_of(ci * rows, rows), rows), :] = (
+                acc[which, j] + partial(ci, oy, j)
+            ).astype(jnp.bfloat16)
+
+    hits_in.wait()
+    for copy in weight_in[0]:
+        copy.wait()
+    got(i, t_partner, 0)
+    got(i, t_partner, 1)
+    open_rows(i, 0)
+
+    got(oi, t, 0)
+    forward(oi, t, 0, y_peer)
+    forward(oi, t, 0, partner)
+    got(i, t_y, 1)
+    forward(i, t_y, 1, x_peer)
+    forward(i, t_y, 1, partner)
+    got(oi, t, 1)
+    forward(oi, t, 1, partner)
+    got(i, t_y, 0)
+    forward(i, t_y, 0, partner)
+
+    got(oi, t_partner, 0)
+    got(oi, t_partner, 1)
+    open_rows(oi, 1)
+
+    got(oi, t_y, 0)
+    forward(oi, t_y, 0, partner)
+    got(oi, t_y, 1)
+    forward(oi, t_y, 1, partner)
+
+    for copy in weight_in[1]:
+        copy.wait()
+    got(i, t_diag_partner, 0)
+    got(i, t_diag_partner, 1)
+    close_rows(i, 0)
+    got(oi, t_diag_partner, 0)
+    got(oi, t_diag_partner, 1)
+    close_rows(oi, 1)
+
+    qrows[...] = jnp.dot(pick[...], proj[0], preferred_element_type=jnp.float32)
+    head_of = lax.broadcasted_iota(jnp.int32, (quarter, width), 1) // HEAD_DIM
+
+    def attend(owner):
+        start = pl.multiple_of(owner * quarter, quarter)
+        queries = qrows[pl.ds(start, quarter), :]
+        spread = jnp.concatenate(
+            [jnp.where(head_of == h, queries, 0.0) for h in range(heads)], axis=0
+        ).astype(jnp.bfloat16)
+        scores = lax.dot_general(
+            spread, proj[1], (((1,), (1,)), ((), ())), preferred_element_type=jnp.float32
+        )
+        allowed = bias[pl.ds(start, quarter), :]
+        scores = scores + jnp.concatenate([allowed] * heads, axis=0)
+        weights = jnp.exp(scores - jnp.max(scores, axis=1, keepdims=True))
+        total = jnp.sum(weights, axis=1, keepdims=True)
+        summed = jnp.dot(
+            weights.astype(jnp.bfloat16), proj[2], preferred_element_type=jnp.float32
+        ) / total
+        merged = jnp.zeros((quarter, width), jnp.float32)
+        for h in range(heads):
+            merged = jnp.where(head_of == h, summed[h * quarter : (h + 1) * quarter], merged)
+        return merged.astype(jnp.bfloat16)
+
+    att_send[0] = attend(t_diag_partner)
+    remote(att_send.at[0], att_recv.at[0], att_sem.at[0], partner)
+    far_mine = attend(t_y)
+    wout_in.wait()
+    far_part = jnp.dot(far_mine, wmine[...], preferred_element_type=jnp.float32)
+    arrived(wtheirs, wout_sem.at[0])
+    arrived(att_recv.at[0], att_sem.at[0])
+    far_send[...] = (
+        far_part + jnp.dot(att_recv[0], wtheirs[...], preferred_element_type=jnp.float32)
+    ).astype(jnp.bfloat16)
+    remote(far_send, far_recv, far_sem.at[0], y_peer)
+
+    att_send[1] = attend(t_partner)
+    remote(att_send.at[1], att_recv.at[1], att_sem.at[1], partner)
+    near[...] = jnp.dot(attend(t), wmine[...], preferred_element_type=jnp.float32)
+    arrived(att_recv.at[1], att_sem.at[1])
+    near[...] += jnp.dot(att_recv[1], wtheirs[...], preferred_element_type=jnp.float32)
+    arrived(far_recv, far_sem.at[0])
+    out_ref[...] = (near[...] + far_recv[...].astype(jnp.float32)).astype(jnp.bfloat16)
+    for copy in sent:
+        copy.wait_send()
+
+
+def small_slice(hits, qkv_weight, out_weight, energy_order, stripe_owner):
+    rows, width = hits.shape
+    model_width = qkv_weight.shape[0]
+    bf16, f32 = jnp.bfloat16, jnp.float32
+    dma = pltpu.SemaphoreType.DMA
+    anywhere = pl.BlockSpec(memory_space=pl.ANY)
+    mixed = pl.pallas_call(
+        layer_kernel,
+        out_shape=jax.ShapeDtypeStruct((rows // 4, model_width), bf16),
+        in_specs=[
+            anywhere,
+            anywhere,
+            anywhere,
+            pl.BlockSpec(memory_space=pltpu.VMEM),
+            pl.BlockSpec(memory_space=pltpu.SMEM),
+        ],
+        out_specs=pl.BlockSpec(memory_space=pltpu.VMEM),
+        scratch_shapes=[
+            pltpu.VMEM((2, 4, rows, width), bf16),
+            pltpu.VMEM((3, model_width, width), bf16),
+            pltpu.VMEM((width, model_width), bf16),
+            pltpu.VMEM((width, model_width), bf16),
+            pltpu.VMEM((2, 3, rows, width), f32),
+            pltpu.VMEM((3, 2 * rows, width), bf16),
+            pltpu.VMEM((rows, 2 * rows), bf16),
+            pltpu.VMEM((rows, 2 * rows), f32),
+            pltpu.VMEM((rows, width), f32),
+            pltpu.VMEM((2, rows // 4, width), bf16),
+            pltpu.VMEM((2, rows // 4, width), bf16),
+            pltpu.VMEM((rows // 4, model_width), bf16),
+            pltpu.VMEM((rows // 4, model_width), bf16),
+            pltpu.VMEM((rows // 4, model_width), f32),
+            dma((8,)),
+            dma((18,)),
+            dma((2, 4, 2)),
+            dma((1,)),
+            dma((2,)),
+            dma((1,)),
+        ],
+        compiler_params=pltpu.CompilerParams(
+            collective_id=0, has_side_effects=True, vmem_limit_bytes=40 * 1024 * 1024
+        ),
+    )(
+        hits,
+        jnp.transpose(qkv_weight, (1, 0, 2)),
+        out_weight,
+        energy_order.reshape(1, -1),
+        stripe_owner,
+    )
+    return mixed[None]
+
+
 def solution(mesh):
+    small = mesh.shape["ctx"] == 2 and mesh.shape["tp"] == 4
     placed = (
         P(("batch", "ctx"), "tp"),
         P(None, None, "tp"),
@@ -201,7 +488,7 @@
         P("batch", None),
     )
     return jax.shard_map(
-        shards,
+        small_slice if small else shards,
         mesh=mesh,
         in_specs=placed,
         out_specs=P(("batch", "ctx"), "tp", None),

time: 79.2 us -> 25.5 us (0.32)
  waiting for transfers between devices: 27.8 us -> 0 us
  Pallas kernels: 0 us -> 19.8 us
  between operations: 16.3 us -> 0.01 us
  blocking collectives: 7.91 us -> 0 us
  local copies, waits for them, and re-layouts: 13.1 us -> 5.37 us
  starting transfers between devices: 6.22 us -> 0 us
  other arithmetic: 3.88 us -> 0 us
  matrix products: 3.68 us -> 0 us
    reduce_scatter x1 -> x0, waiting for transfers between devices: 22.6 us -> none  [shards(): lax.psum_scatter(jnp.dot(merged, out_weight, preferred_element_type=jnp.f...]
    pallas_call x0 -> x1, Pallas kernels: none -> 19.8 us  [small_slice(): pl.pallas_call(layer_kernel, out_shape=jax.ShapeDtypeStruct((rows // 4, m...]
    gather x5 -> x0, local copies, waits for them, and re-layouts: 8.49 us -> none  [the longest x2 3.51 us: routing(): detector = energy_order[every_row]]
    all_gather x1 -> x0, blocking collectives: 7.91 us -> none  [shards(): lax.all_gather(arranged, 'tp', axis=1, tiled=True)]
    ppermute x1 -> x0, waiting for transfers between devices: 5.22 us -> none  [passed_along(): lax.ppermute(shard, axis, [(i, (i + by) % peers) for i in range(peers)])]
    all_to_all x1 -> x0, starting transfers between devices: 4.23 us -> none  [shards(): lax.all_to_all(outgoing, 'ctx', split_axis=0, concat_axis=0, tiled=True)]
    dot_general x10 -> x0, matrix products: 3.68 us -> none  [the longest x1 1.12 us: shards(): jnp.dot(merged, out_weight, preferred_element_type=jnp.float32)]
    unnamed x15 -> x11, local copies, waits for them, and re-layouts: 1.8 us -> 5.37 us
  transfers between devices with their start and end apart: 3 -> 0, of which waited for: 2 -> 0; matrix products, arithmetic and copies ran while one was open for 6% -> 0% of each run, Pallas kernels for 0% -> 0%
where the time goes in v1:
time: 25.5 us; the launch traced here: 25.2 us
  Pallas kernels  19.8 us (78%)
  local copies, waits for them, and re-layouts  5.37 us (21%)
    pallas_call x1, Pallas kernels, small_slice(): pl.pallas_call(layer_kernel, out_shape=jax.ShapeDtypeStruct((rows // 4, m...  19.8 us
    unnamed x11, local copies, waits for them, and re-layouts  5.37 us

profile of v1, /device:TPU:0, one launch (start us, length us, event | category | flops | bytes accessed | tf_op | source)
XLA Modules:
  0.0 25.2 jit_solution(10836389858123461110)
XLA Ops:
  0.0 0.0 copy-start
  0.0 1.4 %copy-done = bf16[1024,3,256]{2,0,1:T(8,128)(2,1)S(1)} copy-done((bf16[1024,3,256]{2,0,1:T(8,128)(2,1)S(1)}, bf16[1024,3,256]{2,0,1:T(8,128)(2,1)}, u32[]{:S(2)}) %copy-start) | copy-done | bytes 1572888
  1.4 0.0 copy-start.1
  1.4 1.0 %copy-done.1 = bf16[256,1024]{1,0:T(8,128)(2,1)S(1)} copy-done((bf16[256,1024]{1,0:T(8,128)(2,1)S(1)}, bf16[256,1024]{1,0:T(8,128)(2,1)}, u32[]{:S(2)}) %copy-start.1) | copy-done | bytes 524312
  2.5 0.0 copy-start.2
  2.5 0.9 %copy-done.2 = bf16[256,256]{1,0:T(8,128)(2,1)S(1)} copy-done((bf16[256,256]{1,0:T(8,128)(2,1)S(1)}, bf16[256,256]{1,0:T(8,128)(2,1)}, u32[]{:S(2)}) %copy-start.2) | copy-done | bytes 131096
  3.4 0.0 copy-start.3
  3.4 0.7 %copy-done.3 = s32[512]{0:T(512)S(1)} copy-done((s32[512]{0:T(512)S(1)}, s32[512]{0:T(512)}, u32[]{:S(2)}) %copy-start.3) | copy-done | bytes 2072
  4.0 0.0 copy-start.4
  4.0 0.7 %copy-done.4 = s32[2,2]{1,0:T(2,128)S(1)} copy-done((s32[2,2]{1,0:T(2,128)S(1)}, s32[2,2]{1,0:T(2,128)}, u32[]{:S(2)}) %copy-start.4) | copy-done | bytes 40
  4.7 19.8 %shard_map.55 = bf16[64,1024]{1,0:T(8,128)(2,1)S(1)} custom-call(bf16[256,256]{1,0:T(8,128)(2,1)S(1)} %copy-done.2, bf16[3,1024,256]{2,1,0:T(8,128)(2,1)S(1)} %bitcast.3, bf16[256,1024]{1,0:T(8,128)(2,1)S(1)} %copy-done.1, s32[1,512]{1,0:T(1,128)S(1)} %bitcast.5, s32[2,2]{1,0:T(2,128)S(1)} %copy-done.4), custom_call_target="tpu_custom_call" | custom-call | tf_op jit(solution)/shard_map/pallas_call | solution.py:435
  24.6 0.7 %copy.7 = bf16[1,64,1024]{2,1,0:T(8,128)(2,1)} copy(bf16[1,64,1024]{2,1,0:T(8,128)(2,1)S(1)} %bitcast.4) | data formatting | bytes 262144
Async XLA Ops:
  0.0 1.4 %copy-start = (bf16[1024,3,256]{2,0,1:T(8,128)(2,1)S(1)}, bf16[1024,3,256]{2,0,1:T(8,128)(2,1)}, u32[]{:S(2)}) copy-start(bf16[1024,3,256]{2,0,1:T(8,128)(2,1)} %param.6) | copy-start | bytes 4718596
  1.4 1.0 %copy-start.1 = (bf16[256,1024]{1,0:T(8,128)(2,1)S(1)}, bf16[256,1024]{1,0:T(8,128)(2,1)}, u32[]{:S(2)}) copy-start(bf16[256,1024]{1,0:T(8,128)(2,1)} %wout_ref.1) | copy-start | bytes 1572868
  2.5 0.9 %copy-start.2 = (bf16[256,256]{1,0:T(8,128)(2,1)S(1)}, bf16[256,256]{1,0:T(8,128)(2,1)}, u32[]{:S(2)}) copy-start(bf16[256,256]{1,0:T(8,128)(2,1)} %hits_ref.1) | copy-start | bytes 393220
  3.4 0.7 %copy-start.3 = (s32[512]{0:T(512)S(1)}, s32[512]{0:T(512)}, u32[]{:S(2)}) copy-start(s32[512]{0:T(512)} %param.8) | copy-start | bytes 6148
  4.0 0.7 %copy-start.4 = (s32[2,2]{1,0:T(2,128)S(1)}, s32[2,2]{1,0:T(2,128)}, u32[]{:S(2)}) copy-start(s32[2,2]{1,0:T(2,128)} %owner_ref.1) | copy-start | bytes 52

commit v2 on v1

--- a/solution.py
+++ b/solution.py
@@ -198,9 +198,11 @@
     hits_ref,
     qkv_ref,
     wout_ref,
+    order_hbm,
+    owner_hbm,
+    out_ref,
     order_ref,
     owner_ref,
-    out_ref,
     gath,
     wq,
     wmine,
@@ -249,6 +251,8 @@
         return copy
 
     hits_in = local_copy(hits_ref, gath.at[i, t])
+    order_in = local_copy(order_hbm, order_ref)
+    owner_in = local_copy(owner_hbm, owner_ref)
     weight_in = [
         [
             local_copy(
@@ -312,6 +316,8 @@
     own_to(0, y_peer)
     remote(wout_ref, wtheirs, wout_sem.at[0], partner)
 
+    order_in.wait()
+    owner_in.wait()
     order = order_ref[...].astype(jnp.float32)
     order_rows = jnp.transpose(jnp.broadcast_to(order, (128, seq)))
     entry = lax.broadcasted_iota(jnp.int32, (seq, 128), 0).astype(jnp.float32)
@@ -431,19 +437,21 @@
     model_width = qkv_weight.shape[0]
     bf16, f32 = jnp.bfloat16, jnp.float32
     dma = pltpu.SemaphoreType.DMA
-    anywhere = pl.BlockSpec(memory_space=pl.ANY)
+    in_hbm = pl.BlockSpec(memory_space=pl.ANY)
     mixed = pl.pallas_call(
         layer_kernel,
         out_shape=jax.ShapeDtypeStruct((rows // 4, model_width), bf16),
         in_specs=[
-            anywhere,
-            anywhere,
-            anywhere,
-            pl.BlockSpec(memory_space=pltpu.VMEM),
-            pl.BlockSpec(memory_space=pltpu.SMEM),
+            in_hbm,
+            in_hbm,
+            in_hbm,
+            in_hbm,
+            in_hbm,
         ],
         out_specs=pl.BlockSpec(memory_space=pltpu.VMEM),
         scratch_shapes=[
+            pltpu.VMEM((1, 2 * rows), jnp.int32),
+            pltpu.SMEM((2, 2), jnp.int32),
             pltpu.VMEM((2, 4, rows, width), bf16),
             pltpu.VMEM((3, model_width, width), bf16),
             pltpu.VMEM((width, model_width), bf16),
@@ -458,7 +466,7 @@
             pltpu.VMEM((rows // 4, model_width), bf16),
             pltpu.VMEM((rows // 4, model_width), bf16),
             pltpu.VMEM((rows // 4, model_width), f32),
-            dma((8,)),
+            dma((10,)),
             dma((18,)),
             dma((2, 4, 2)),
             dma((1,)),
@@ -466,7 +474,7 @@
             dma((1,)),
         ],
         compiler_params=pltpu.CompilerParams(
-            collective_id=0, has_side_effects=True, vmem_limit_bytes=40 * 1024 * 1024
+            collective_id=0, has_side_effects=True, vmem_limit_bytes=67043328
         ),
     )(
         hits,

time: 25.5 us -> 21.5 us (0.84)
  local copies, waits for them, and re-layouts: 5.37 us -> 1.57 us
    unnamed x11 -> x1, local copies, waits for them, and re-layouts: 5.37 us -> 1.57 us
where the time goes in v2:
time: 21.5 us; the launch traced here: 21.4 us
  Pallas kernels  19.8 us (92%)
  local copies, waits for them, and re-layouts  1.57 us (7%)
    pallas_call x1, Pallas kernels, small_slice(): pl.pallas_call(layer_kernel, out_shape=jax.ShapeDtypeStruct((rows // 4, m...  19.8 us
    unnamed x1, local copies, waits for them, and re-layouts  1.57 us

profile of v2, /device:TPU:0, one launch (start us, length us, event | category | flops | bytes accessed | tf_op | source)
XLA Modules:
  0.0 21.4 jit_solution(11458766822164751358)
XLA Ops:
  0.0 19.8 %shard_map.55 = bf16[64,1024]{1,0:T(8,128)(2,1)} custom-call(bf16[256,256]{1,0:T(8,128)(2,1)} %hits_ref.1, bf16[3,1024,256]{2,1,0:T(8,128)(2,1)} %bitcast.3, bf16[256,1024]{1,0:T(8,128)(2,1)} %wout_ref.1, s32[1,512]{1,0:T(1,128)} %bitcast.5, s32[2,2]{1,0:T(2,128)} %owner_hbm.1), custom_call_target="tpu_custom_call" | custom-call | tf_op jit(solution)/shard_map/pallas_call | solution.py:441
  19.8 1.6 %copy.7 = bf16[1,64,1024]{2,1,0:T(8,128)(2,1)} copy(bf16[1,64,1024]{2,1,0:T(8,128)(2,1)} %bitcast.4) | data formatting | bytes 262144

commit v3 on v2

--- a/solution.py
+++ b/solution.py
@@ -242,6 +242,12 @@
     t_y = 2 * oy + c
     t_diag_partner = 2 * oy + 1 - c
 
+    barrier = pltpu.get_barrier_semaphore()
+    for peer in (partner, x_peer, y_peer):
+        pl.semaphore_signal(
+            barrier, inc=1, device_id=peer, device_id_type=pl.DeviceIdType.MESH
+        )
+
     local = []
 
     def local_copy(src, dst):
@@ -265,11 +271,6 @@
     ]
     wout_in = local_copy(wout_ref, wmine)
 
-    barrier = pltpu.get_barrier_semaphore()
-    for peer in (partner, x_peer, y_peer):
-        pl.semaphore_signal(
-            barrier, inc=1, device_id=peer, device_id_type=pl.DeviceIdType.MESH
-        )
     pl.semaphore_wait(barrier, 3)
 
     sent = []
@@ -440,7 +441,7 @@
     in_hbm = pl.BlockSpec(memory_space=pl.ANY)
     mixed = pl.pallas_call(
         layer_kernel,
-        out_shape=jax.ShapeDtypeStruct((rows // 4, model_width), bf16),
+        out_shape=pltpu.VMEM((rows // 4, model_width), bf16),
         in_specs=[
             in_hbm,
             in_hbm,
@@ -474,7 +475,7 @@
             dma((1,)),
         ],
         compiler_params=pltpu.CompilerParams(
-            collective_id=0, has_side_effects=True, vmem_limit_bytes=67043328
+            collective_id=0, has_side_effects=True, vmem_limit_bytes=64000000
         ),
     )(
         hits,

time: 21.5 us -> 20 us (0.930)
  local copies, waits for them, and re-layouts: 1.57 us -> 0.66 us
  Pallas kernels: 19.8 us -> 19.1 us
    unnamed x1, local copies, waits for them, and re-layouts: 1.57 us -> 0.66 us
    pallas_call x1, Pallas kernels: 19.8 us -> 19.1 us  [small_slice(): pl.pallas_call(layer_kernel, out_shape=pltpu.VMEM((rows // 4, model_width...]
where the time goes in v3:
time: 20 us; the launch traced here: 19.8 us
  Pallas kernels  19.1 us (96%)
  local copies, waits for them, and re-layouts  0.66 us (3%)
    pallas_call x1, Pallas kernels, small_slice(): pl.pallas_call(layer_kernel, out_shape=pltpu.VMEM((rows // 4, model_width...  19.1 us
    unnamed x1, local copies, waits for them, and re-layouts  0.66 us

profile of v3, /device:TPU:0, one launch (start us, length us, event | category | flops | bytes accessed | tf_op | source)
XLA Modules:
  0.0 19.8 jit_solution(10235849751946856637)
XLA Ops:
  0.0 19.1 %shard_map.55 = bf16[64,1024]{1,0:T(8,128)(2,1)S(1)} custom-call(bf16[256,256]{1,0:T(8,128)(2,1)} %hits_ref.1, bf16[3,1024,256]{2,1,0:T(8,128)(2,1)} %bitcast.4, bf16[256,1024]{1,0:T(8,128)(2,1)} %wout_ref.1, s32[1,512]{1,0:T(1,128)} %bitcast.5, s32[2,2]{1,0:T(2,128)} %owner_hbm.1), custom_call_target="tpu_custom_call" | custom-call | tf_op jit(solution)/shard_map/pallas_call | solution.py:442
  19.2 0.7 %copy.7 = bf16[1,64,1024]{2,1,0:T(8,128)(2,1)} copy(bf16[1,64,1024]{2,1,0:T(8,128)(2,1)S(1)} %bitcast.3) | data formatting | bytes 262144

commit v4 on v3

--- a/solution.py
+++ b/solution.py
@@ -260,13 +260,10 @@
     order_in = local_copy(order_hbm, order_ref)
     owner_in = local_copy(owner_hbm, owner_ref)
     weight_in = [
-        [
-            local_copy(
-                qkv_ref.at[j, pl.ds(part * 2 * width, 2 * width)],
-                wq.at[j, pl.ds(part * 2 * width, 2 * width)],
-            )
-            for j in range(3)
-        ]
+        local_copy(
+            qkv_ref.at[:, pl.ds(part * 2 * width, 2 * width)],
+            wq.at[:, pl.ds(part * 2 * width, 2 * width)],
+        )
         for part in (y, oy)
     ]
     wout_in = local_copy(wout_ref, wmine)
@@ -297,24 +294,32 @@
             device_id_type=pl.DeviceIdType.MESH,
         ).wait_recv()
 
-    def slot(ci, ti, h):
-        return gath.at[ci, ti, pl.ds(h * half, half)]
-
-    def own_to(h, peer):
-        remote(hits_ref.at[pl.ds(h * half, half)], slot(i, t, h), gath_sem.at[i, t, h], peer)
-
-    def forward(ci, ti, h, peer):
-        remote(slot(ci, ti, h), slot(ci, ti, h), gath_sem.at[ci, ti, h], peer)
-
-    def got(ci, ti, h):
-        arrived(slot(ci, ti, h), gath_sem.at[ci, ti, h])
-
-    own_to(0, x_peer)
-    own_to(1, y_peer)
-    own_to(0, partner)
-    own_to(1, partner)
-    own_to(1, x_peer)
-    own_to(0, y_peer)
+    first, second, third, fourth = ((k * quarter, quarter) for k in range(4))
+    low, high, whole = (0, half), (half, half), (0, rows)
+    chunk_sem = {first: 0, second: 1, third: 2, fourth: 3, low: 0, high: 2, whole: 0}
+
+    def slot(ci, ti, chunk):
+        return gath.at[ci, ti, pl.ds(*chunk)], gath_sem.at[ci, ti, chunk_sem[chunk]]
+
+    def own_to(peer, chunk):
+        remote(hits_ref.at[pl.ds(*chunk)], *slot(i, t, chunk), peer)
+
+    def forward(ci, ti, chunk, *peers):
+        arrived(*slot(ci, ti, chunk))
+        for peer in peers:
+            remote(slot(ci, ti, chunk)[0], *slot(ci, ti, chunk), peer)
+
+    def got(ci, ti, *chunks):
+        for chunk in chunks:
+            arrived(*slot(ci, ti, chunk))
+
+    own_to(x_peer, first)
+    own_to(y_peer, fourth)
+    own_to(x_peer, second)
+    own_to(y_peer, third)
+    own_to(partner, whole)
+    own_to(x_peer, high)
+    own_to(y_peer, low)
     remote(wout_ref, wtheirs, wout_sem.at[0], partner)
 
     order_in.wait()
@@ -324,8 +329,8 @@
     entry = lax.broadcasted_iota(jnp.int32, (seq, 128), 0).astype(jnp.float32)
     lane = lax.broadcasted_iota(jnp.int32, (seq, 128), 1)
     row = lax.broadcasted_iota(jnp.int32, (rows, 128), 0)
-    first, second = owner_ref[i, 0], owner_ref[i, 1]
-    mine_pos = jnp.where(row < half, first * half + row, second * half + row - half).astype(
+    stripe_a, stripe_b = owner_ref[i, 0], owner_ref[i, 1]
+    mine_pos = jnp.where(row < half, stripe_a * half + row, stripe_b * half + row - half).astype(
         jnp.float32
     )
     for block in range(seq // 128):
@@ -351,39 +356,31 @@
             ).astype(jnp.bfloat16)
 
     hits_in.wait()
-    for copy in weight_in[0]:
-        copy.wait()
-    got(i, t_partner, 0)
-    got(i, t_partner, 1)
+    weight_in[0].wait()
+    got(i, t_partner, whole)
     open_rows(i, 0)
 
-    got(oi, t, 0)
-    forward(oi, t, 0, y_peer)
-    forward(oi, t, 0, partner)
-    got(i, t_y, 1)
-    forward(i, t_y, 1, x_peer)
-    forward(i, t_y, 1, partner)
-    got(oi, t, 1)
-    forward(oi, t, 1, partner)
-    got(i, t_y, 0)
-    forward(i, t_y, 0, partner)
-
-    got(oi, t_partner, 0)
-    got(oi, t_partner, 1)
+    forward(oi, t, first, y_peer)
+    forward(i, t_y, fourth, x_peer)
+    forward(oi, t, second, y_peer)
+    forward(i, t_y, third, x_peer)
+    remote(slot(oi, t, low)[0], *slot(oi, t, low), partner)
+    remote(slot(i, t_y, high)[0], *slot(i, t_y, high), partner)
+    forward(oi, t, high, partner)
+    forward(i, t_y, low, partner)
+
+    got(oi, t_partner, low, high)
     open_rows(oi, 1)
 
-    got(oi, t_y, 0)
-    forward(oi, t_y, 0, partner)
-    got(oi, t_y, 1)
-    forward(oi, t_y, 1, partner)
-
-    for copy in weight_in[1]:
-        copy.wait()
-    got(i, t_diag_partner, 0)
-    got(i, t_diag_partner, 1)
+    forward(oi, t_y, first, partner)
+    forward(oi, t_y, fourth, partner)
+    forward(oi, t_y, second, partner)
+    forward(oi, t_y, third, partner)
+
+    weight_in[1].wait()
+    got(i, t_diag_partner, low, high)
     close_rows(i, 0)
-    got(oi, t_diag_partner, 0)
-    got(oi, t_diag_partner, 1)
+    got(oi, t_diag_partner, first, fourth, second, third)
     close_rows(oi, 1)
 
     qrows[...] = jnp.dot(pick[...], proj[0], preferred_element_type=jnp.float32)
@@ -417,20 +414,28 @@
     far_part = jnp.dot(far_mine, wmine[...], preferred_element_type=jnp.float32)
     arrived(wtheirs, wout_sem.at[0])
     arrived(att_recv.at[0], att_sem.at[0])
-    far_send[...] = (
-        far_part + jnp.dot(att_recv[0], wtheirs[...], preferred_element_type=jnp.float32)
-    ).astype(jnp.bfloat16)
-    remote(far_send, far_recv, far_sem.at[0], y_peer)
+    cut = far_send.shape[1] // 2
+    for side in range(2):
+        cols = slice(side * cut, (side + 1) * cut)
+        far_send[:, cols] = (
+            far_part[:, cols]
+            + jnp.dot(att_recv[0], wtheirs[:, cols], preferred_element_type=jnp.float32)
+        ).astype(jnp.bfloat16)
+        remote(far_send.at[:, cols], far_recv.at[:, cols], far_sem.at[side], y_peer)
 
     att_send[1] = attend(t_partner)
     remote(att_send.at[1], att_recv.at[1], att_sem.at[1], partner)
     near[...] = jnp.dot(attend(t), wmine[...], preferred_element_type=jnp.float32)
     arrived(att_recv.at[1], att_sem.at[1])
     near[...] += jnp.dot(att_recv[1], wtheirs[...], preferred_element_type=jnp.float32)
-    arrived(far_recv, far_sem.at[0])
-    out_ref[...] = (near[...] + far_recv[...].astype(jnp.float32)).astype(jnp.bfloat16)
     for copy in sent:
         copy.wait_send()
+    for side in range(2):
+        cols = slice(side * cut, (side + 1) * cut)
+        arrived(far_recv.at[:, cols], far_sem.at[side])
+        out_ref[:, cols] = (near[:, cols] + far_recv[:, cols].astype(jnp.float32)).astype(
+            jnp.bfloat16
+        )
 
 
 def small_slice(hits, qkv_weight, out_weight, energy_order, stripe_owner):
@@ -467,12 +472,12 @@
             pltpu.VMEM((rows // 4, model_width), bf16),
             pltpu.VMEM((rows // 4, model_width), bf16),
             pltpu.VMEM((rows // 4, model_width), f32),
-            dma((10,)),
-            dma((18,)),
-            dma((2, 4, 2)),
+            dma((6,)),
+            dma((24,)),
+            dma((2, 4, 4)),
             dma((1,)),
             dma((2,)),
-            dma((1,)),
+            dma((2,)),
         ],
         compiler_params=pltpu.CompilerParams(
             collective_id=0, has_side_effects=True, vmem_limit_bytes=64000000

time: 20 us -> 19.6 us (0.980)
  Pallas kernels: 19.1 us -> 18.8 us
    pallas_call x1, Pallas kernels: 19.1 us -> 18.8 us  [small_slice(): pl.pallas_call(layer_kernel, out_shape=pltpu.VMEM((rows // 4, model_width...]
where the time goes in v4:
time: 19.6 us; the launch traced here: 19.5 us
  Pallas kernels  18.8 us (96%)
  local copies, waits for them, and re-layouts  0.66 us (3%)
    pallas_call x1, Pallas kernels, small_slice(): pl.pallas_call(layer_kernel, out_shape=pltpu.VMEM((rows // 4, model_width...  18.8 us
    unnamed x1, local copies, waits for them, and re-layouts  0.66 us

profile of v4, /device:TPU:0, one launch (start us, length us, event | category | flops | bytes accessed | tf_op | source)
XLA Modules:
  0.0 19.5 jit_solution(9983386990832355593)
XLA Ops:
  0.0 18.8 %shard_map.55 = bf16[64,1024]{1,0:T(8,128)(2,1)S(1)} custom-call(bf16[256,256]{1,0:T(8,128)(2,1)} %hits_ref.1, bf16[3,1024,256]{2,1,0:T(8,128)(2,1)} %bitcast.4, bf16[256,1024]{1,0:T(8,128)(2,1)} %wout_ref.1, s32[1,512]{1,0:T(1,128)} %bitcast.5, s32[2,2]{1,0:T(2,128)} %owner_hbm.1), custom_call_target="tpu_custom_call" | custom-call | tf_op jit(solution)/shard_map/pallas_call | solution.py:447
  18.8 0.7 %copy.7 = bf16[1,64,1024]{2,1,0:T(8,128)(2,1)} copy(bf16[1,64,1024]{2,1,0:T(8,128)(2,1)S(1)} %bitcast.3) | data formatting | bytes 262144
